TPU v7x, 512 devices: a whole 4x8x8 slice. The times are simulated.
512 devices in a mesh: sta: 64 (over y, x, z_hi), win: 8 (over z_lo, core).
Axes of the slice: x: 4, y: 8, z: 8 (z_hi: 2, z_lo: 4; z = z_hi * 4 + z_lo), core: 2. Of those that a mesh axis runs over, the one named last changes fastest.
Arguments:
- spectra: float32 [16, 256, 2, 3, 1664], P('win', 'sta')
- flags: int32 [16, 256], P('win', 'sta'), may hold values 0 or 1
- owners: int32 [4], replicated, may hold values from 0 to 63, as said below
- source_slots: int32 [4, 4], replicated, may hold values from 0 to 3, as said below
Outputs:
- correlations: float32 [4, 4, 3, 256, 3, 768], P(None, None, None, 'sta')
Inputs may be any that keep to these rules, and one draw needn't show every extreme that they name: `owners`: the index of a block of 4 stations along sta. `source_slots`: distinct within a step.
All inputs are finite; a program needn't handle non-finite values. No bound on the sum of `flags` on one device may be relied on, other than what follows from the above.
Results may differ from a plain program's by a relative error of at most 0.0037.
Values sent between devices are 32-bit elements; how exact they have to be, the bound alone decides.
A program may use at most 64 MiB of HBM per device.

v0:
```python
import math
import jax
import jax.numpy as jnp
from jax import lax
from jax.sharding import PartitionSpec as P

NLAG = 768
STEPS = 4


def spread(value, axis, source):
    kept = jnp.where(lax.axis_index(axis) == source, value, 0).astype(value.dtype)
    return lax.psum(kept, axis)


def whiten(spectra):
    shape = spectra.shape
    blocks = spectra.reshape(shape[0], shape[1], 2, 3, shape[4] // 64, 64)
    power = jnp.mean(blocks * blocks, axis=(2, 3, 5), keepdims=True)
    return (blocks / jnp.sqrt(power + 1e-06)).reshape(shape)


def lag_table(bins, lags, windows):
    freq = jnp.arange(bins, dtype=jnp.int32) + 360
    shift = jnp.arange(lags, dtype=jnp.int32) - lags // 2
    phase = jnp.mod(freq[:, None] * shift[None, :], 7200).astype(jnp.float32) * (
        2.0 * math.pi / 7200.0
    )
    scale = 1.0 / math.sqrt(windows * bins)
    return jnp.concatenate([jnp.cos(phase) * scale, -jnp.sin(phase) * scale], axis=0).astype(
        jnp.bfloat16
    )


def correlate(picked, receivers, table):
    src_re = picked[:, :, 0][:, :, :, None, None, :]
    src_im = picked[:, :, 1][:, :, :, None, None, :]
    rec_re = receivers[:, :, 0][:, None, None, :, :, :]
    rec_im = receivers[:, :, 1][:, None, None, :, :, :]
    real = jnp.sum(src_re * rec_re + src_im * rec_im, axis=0)
    imag = jnp.sum(src_im * rec_re - src_re * rec_im, axis=0)
    shape = real.shape
    bins = shape[4]
    rows = jnp.concatenate([real.reshape(-1, bins), imag.reshape(-1, bins)], axis=1).astype(
        jnp.bfloat16
    )
    lagged = jnp.dot(rows, table, preferred_element_type=jnp.float32)
    return lagged.reshape(shape[0], shape[1], shape[2], shape[3], table.shape[1])


def on_device(spectra, flags, owners, source_slots):
    win_count = spectra.shape[0]
    bins = spectra.shape[4]
    weighted = whiten(spectra) * flags.astype(jnp.float32)[:, :, None, None, None]
    table = lag_table(bins, NLAG, win_count * lax.axis_size("win"))
    outputs = []
    for step in range(STEPS):
        chosen = jnp.take(weighted, source_slots[step], axis=1)
        picked = spread(chosen, "sta", owners[step])
        partial_stack = correlate(picked, weighted, table)
        partial_stack = lax.psum(partial_stack, "win")
        outputs.append(partial_stack)
    stacked = jnp.stack(outputs)
    return stacked


def solution(mesh):
    return jax.shard_map(
        on_device,
        mesh=mesh,
        in_specs=(P("win", "sta", None, None, None), P("win", "sta"), P(), P()),
        out_specs=P(None, None, None, "sta", None, None),
        check_vma=False,
    )
```

profile of v0, /device:TPU:2, one launch (start us, length us, event | category | flops | bytes accessed | tf_op | source)
XLA Modules:
  0.0 1011.2 jit_solution(12105499621488720330)
XLA Ops:
  6.5 0.7 convert_element_type.18
  7.2 1.5 fusion.30
  11.2 0.8 compare_and_fusion
  12.1 1.2 multiply_reduce_fusion
  13.3 0.1 reduce_sum.89
  13.4 0.1 reduce_sum.90
  13.8 1.1 divide_multiply_fusion
  14.9 0.9 gather_fusion.2
  15.9 0.9 gather_fusion.1
  16.8 0.9 gather_fusion.3
  17.7 0.9 gather_fusion
  18.6 1.2 bitcast_select_fusion
  19.8 1.2 bitcast_select_fusion.2
  21.2 0.2 fusion.29
  21.5 23.4 %multiply_convert_fusion.1 = (bf16[1664,768]{1,0:T(8,128)(2,1)S(1)}, bf16[1664,768]{1,0:T(8,128)(2,1)}) fusion(s32[768]{0:T(1024)S(1)} %iota_add_fusion.1, s32[1664]{0:T(1024)S(1)} %iota_add_fusion), kind=kLoop, calls=%fused_computation.9 | loop fusion | flops 17891328 | bytes 5121536 | tf_op jit(solution)/shard_map/convert.12
  45.0 813.5 %all-reduce.5.cloned.1.call-done = (f32[2,4,2,3,1664]{4,2,3,0,1:T(2,128)}, f32[2,4,2,3,1664]{4,2,3,0,1:T(2,128)}, f32[2,4,2,3,1664]{4,2,3,0,1:T(2,128)}, f32[2,4,2,3,1664]{4,2,3,0,1:T(2,128)}) async-done(((f32[2,4,2,3,1664]{4,2,3,0,1:T(2,128)}, f32[2,4,2,3,1664]{4,2,3,0,1:T(2,128)}, f32[2,4,2,3,1664]{4,2,3,0,1:T(2,128)}, f32[2,4,2,3,1664]{4,2,3,0,1:T(2,128)}), (f32[2,4,2,3,1664]{4,2,3,0,1:T(2,128)}, ...) | async-done | bytes 1277968 | tf_op jit(solution)/shard_map/psum | solution.py:13
  858.4 1.4 fusion.28
  860.0 1.3 fusion.27
  861.5 0.2 fusion.26
  861.8 0.2 fusion.25
  862.2 14.1 %add_reduce_fusion.3 = (bf16[4,3,4,3,1664]{4,2,3,1,0:T(4,128)(2,1)S(1)}, bf16[4,3,4,3,1664]{4,2,3,1,0:T(4,128)(2,1)}, bf16[4,3,4,3,1664]{4,2,3,1,0:T(4,128)(2,1)...) fusion(f32[2,4,3,1664]{3,1,2,0:T(4,128)S(1)} %get-tuple-element, ...), kind=kLoop, calls=%fused_computation.22 | loop fusion | flops 13418496 | bytes 5431296 | tf_op jit(solution)/shard_map/reduce_sum | solution.py:40
  876.4 0.2 copy.44
  876.6 1.2 reshape.80
  877.8 1.3 copy.45
  879.1 1.2 reshape.81
  880.2 1.3 copy.51
  881.5 1.2 reshape.84
  882.7 1.3 copy.50
  884.0 1.2 reshape.83
  885.1 1.3 copy.57
  886.4 1.2 reshape.87
  887.6 1.3 copy.56
  888.9 1.2 reshape.86
  890.1 1.3 copy.63
  891.3 1.2 reshape.90
  892.5 1.3 copy.62
  893.8 1.2 reshape.89
  895.0 3.8 fusion.5
  898.8 2.0 stack.15
  900.8 3.4 fusion.17
  904.2 2.0 stack.18
  906.2 3.8 fusion.13
  910.0 2.0 stack.17
  912.0 3.4 fusion.9
  915.5 2.0 stack.16
  917.5 83.0 %all-reduce.7.cloned.1.call-done = (f32[1,4,3,4,3,768]{5,4,3,2,1,0:T(4,128)}, f32[1,4,3,4,3,768]{5,4,3,2,1,0:T(4,128)}, f32[1,4,3,4,3,768]{5,4,3,2,1,0:T(4,128)}, f32[1,4,3,4,3,768]{5,4,3,2,1,0:T(4,128)}) async-done(((f32[1,4,3,4,3,768]{5,4,3,2,1,0:T(4,128)}, f32[1,4,3,4,3,768]{5,4,3,2,1,0:T(4,128)}, f32[1,4,3,4,3,768]{5,4,3,2,1,0:T(4,128)}, f32[1,4,3,4,3,768]{5,4,3,2,1,0:T(4,128)}), ...) | async-done | bytes 1769488 | tf_op jit(solution)/shard_map/psum | solution.py:61
  1000.5 2.2 pad_maximum_fusion.1
  1002.7 1.7 copy.64
  (34 shorter events, 0.9 us)
Async XLA Ops:
  6.5 851.9 %all-reduce.5.cloned.1.call-start = ((), (), s32[]{:S(2)}) async-start(), calls=%async_computation | async-start | bytes 2555904 | tf_op jit(solution)/shard_map/psum | solution.py:13
  21.1 979.4 %all-reduce.7.cloned.1.call-start = ((), (), s32[]{:S(2)}) async-start(), calls=%async_computation.1 | async-start | bytes 4718592 | tf_op jit(solution)/shard_map/psum | solution.py:61
  858.4 3.0 copy-start.5
  858.4 3.4 copy-start.4
  895.0 5.8 copy-start.2
  895.0 5.8 copy-start.3
  906.2 5.8 copy-start
  906.2 5.8 copy-start.1
Sparse Core Ops, SparseCore 0:
  21.2 837.1 all-reduce.4
  917.6 82.8 all-reduce.6
where the time goes:
time: 1010 us
  waiting for transfers between devices  896 us (89%)
  other arithmetic  46.3 us (5%)
  local copies, waits for them, and re-layouts  37.7 us (4%)
  between operations  16.2 us (2%)
  matrix products  14.4 us (1%)
    psum x1, waiting for transfers between devices, spread(): return lax.psum(kept, axis)  813 us
    psum x1, waiting for transfers between devices, on_device(): partial_stack = lax.psum(partial_stack, 'win')  83 us
    another operation x1, other arithmetic  23.4 us
  transfers between devices with their start and end apart: 2, of which 2 were waited for; matrix products, arithmetic and copies ran while one was open for 2% of the time, Pallas kernels for 0%

commit v1 on v0

--- a/solution.py
+++ b/solution.py
@@ -58,7 +58,8 @@
         chosen = jnp.take(weighted, source_slots[step], axis=1)
         picked = spread(chosen, "sta", owners[step])
         partial_stack = correlate(picked, weighted, table)
-        partial_stack = lax.psum(partial_stack, "win")
+        shards = lax.all_gather(partial_stack, "win")
+        partial_stack = jnp.sum(shards, axis=0)
         outputs.append(partial_stack)
     stacked = jnp.stack(outputs)
     return stacked

time: 1010 us -> 1100 us (1.089)
  waiting for transfers between devices: 896 us -> 976 us
    all_gather x0 -> x4, waiting for transfers between devices: none -> 163 us  [on_device(): shards = lax.all_gather(partial_stack, 'win')]
    psum x1 -> x0, waiting for transfers between devices: 83 us -> none  [on_device(): partial_stack = lax.psum(partial_stack, 'win')]
  transfers between devices with their start and end apart: 2 -> 5, of which waited for: 2 -> 5; matrix products, arithmetic and copies ran while one was open for 2% -> 6% of each run, Pallas kernels for 0% -> 0%
where the time goes in v1:
time: 1100 us
  waiting for transfers between devices  976 us (89%)
  other arithmetic  55.2 us (5%)
  local copies, waits for them, and re-layouts  38.8 us (4%)
  between operations  16 us (1%)
  matrix products  14.9 us (1%)
    psum x1, waiting for transfers between devices, spread(): return lax.psum(kept, axis)  813 us
    all_gather x4, waiting for transfers between devices, on_device(): shards = lax.all_gather(partial_stack, 'win')  163 us
    another operation x1, other arithmetic  23.5 us
  transfers between devices with their start and end apart: 5, of which 5 were waited for; matrix products, arithmetic and copies ran while one was open for 6% of the time, Pallas kernels for 0%

profile of v1, /device:TPU:2, one launch (start us, length us, event | category | flops | bytes accessed | tf_op | source)
XLA Modules:
  0.0 1101.4 jit_solution(11347958544234967714)
XLA Ops:
  7.2 1.5 fusion.30
  12.1 1.2 multiply_reduce_fusion
  13.8 1.1 divide_multiply_fusion
  14.9 0.9 gather_fusion.2
  15.9 0.9 gather_fusion.1
  16.8 0.9 gather_fusion.3
  17.7 0.9 gather_fusion
  18.6 1.2 bitcast_select_fusion
  19.8 1.2 bitcast_select_fusion.2
  21.7 23.5 %multiply_convert_fusion.1 = (bf16[1664,768]{1,0:T(8,128)(2,1)S(1)}, bf16[1664,768]{1,0:T(8,128)(2,1)}) fusion(s32[768]{0:T(1024)S(1)} %iota_add_fusion.1, s32[1664]{0:T(1024)S(1)} %iota_add_fusion), kind=kLoop, calls=%fused_computation.9 | loop fusion | flops 17891328 | bytes 5121536 | tf_op jit(solution)/shard_map/convert.12
  45.2 812.8 %all-reduce.3.cloned.1.call-done = (f32[2,4,2,3,1664]{4,2,3,0,1:T(2,128)}, f32[2,4,2,3,1664]{4,2,3,0,1:T(2,128)}, f32[2,4,2,3,1664]{4,2,3,0,1:T(2,128)}, f32[2,4,2,3,1664]{4,2,3,0,1:T(2,128)}) async-done(((f32[2,4,2,3,1664]{4,2,3,0,1:T(2,128)}, f32[2,4,2,3,1664]{4,2,3,0,1:T(2,128)}, f32[2,4,2,3,1664]{4,2,3,0,1:T(2,128)}, f32[2,4,2,3,1664]{4,2,3,0,1:T(2,128)}), (f32[2,4,2,3,1664]{4,2,3,0,1:T(2,128)}, ...) | async-done | bytes 1277968 | tf_op jit(solution)/shard_map/psum | solution.py:13
  857.9 1.4 fusion.28
  859.5 1.3 fusion.27
  861.7 13.9 %add_reduce_fusion.3 = (bf16[4,3,4,3,1664]{4,2,3,1,0:T(4,128)(2,1)S(1)}, bf16[4,3,4,3,1664]{4,2,3,1,0:T(4,128)(2,1)}, bf16[4,3,4,3,1664]{4,2,3,1,0:T(4,128)(2,1)...) fusion(f32[2,4,3,1664]{3,1,2,0:T(4,128)S(1)} %get-tuple-element, ...), kind=kLoop, calls=%fused_computation.22 | loop fusion | flops 13418496 | bytes 5431296 | tf_op jit(solution)/shard_map/reduce_sum | solution.py:40
  875.9 1.2 reshape.68
  877.1 1.3 copy.69
  878.4 1.2 reshape.69
  879.6 3.7 fusion.5
  883.3 1.2 all_gather_reshape.12
  885.7 1.3 copy.93
  886.9 1.2 reshape.75
  888.1 1.3 copy.92
  889.4 1.2 reshape.74
  890.6 3.8 fusion.17
  894.4 1.2 all_gather_reshape.15
  895.6 0.9 copy.94
  896.6 1.3 copy.85
  897.9 1.2 reshape.73
  899.0 1.3 copy.84
  900.3 1.2 reshape.72
  901.5 3.7 fusion.13
  905.2 1.2 all_gather_reshape.14
  906.4 0.9 copy.86
  907.4 1.3 copy.77
  908.7 1.2 reshape.71
  909.9 1.3 copy.76
  911.1 1.2 reshape.70
  912.4 3.7 fusion.9
  916.1 1.2 all_gather_reshape.13
  918.2 14.1 %all-gather.5.cloned.1.call-done = f32[8,4,3,4,3,768]{5,3,4,2,1,0:T(4,128)} async-done(((f32[1,4,3,4,3,768]{5,3,4,2,1,0:T(4,128)}), f32[8,4,3,4,3,768]{5,3,4,2,1,0:T(4,128)}) %all-gather.5.cloned.1.call-update) | async-done | bytes 3538960 | tf_op jit(solution)/shard_map/all_gather | solution.py:61
  932.3 2.7 reduce_sum.129
  935.1 49.7 %all-gather.11.cloned.1.call-done = f32[8,4,3,4,3,768]{5,3,4,2,1,0:T(4,128)} async-done(((f32[1,4,3,4,3,768]{5,3,4,2,1,0:T(4,128)}), f32[8,4,3,4,3,768]{5,3,4,2,1,0:T(4,128)}) %all-gather.11.cloned.1.call-update) | async-done | bytes 3538960 | tf_op jit(solution)/shard_map/all_gather | solution.py:61
  984.8 2.7 reduce_sum.138
  987.7 49.6 %all-gather.9.cloned.1.call-done = f32[8,4,3,4,3,768]{5,3,4,2,1,0:T(4,128)} async-done(((f32[1,4,3,4,3,768]{5,3,4,2,1,0:T(4,128)}), f32[8,4,3,4,3,768]{5,3,4,2,1,0:T(4,128)}) %all-gather.9.cloned.1.call-update) | async-done | bytes 3538960 | tf_op jit(solution)/shard_map/all_gather | solution.py:61
  1037.3 2.7 reduce_sum.135
  1040.1 49.6 %all-gather.7.cloned.1.call-done = f32[8,4,3,4,3,768]{5,3,4,2,1,0:T(4,128)} async-done(((f32[1,4,3,4,3,768]{5,3,4,2,1,0:T(4,128)}), f32[8,4,3,4,3,768]{5,3,4,2,1,0:T(4,128)}) %all-gather.7.cloned.1.call-update) | async-done | bytes 3538960 | tf_op jit(solution)/shard_map/all_gather | solution.py:61
  1089.7 2.7 reduce_sum.132
  1093.2 1.7 copy.96
  (47 shorter events, 7.2 us)
Async XLA Ops:
  6.5 851.4 %all-reduce.3.cloned.1.call-start = ((), (), s32[]{:S(2)}) async-start(), calls=%async_computation.4 | async-start | bytes 2555904 | tf_op jit(solution)/shard_map/psum | solution.py:13
  21.1 911.2 %all-gather.5.cloned.1.call-start = ((), (), s32[]{:S(2)}) async-start(), calls=%async_computation | async-start | bytes 3981312 | tf_op jit(solution)/shard_map/all_gather | solution.py:61
  857.9 3.0 copy-start.1
  857.9 3.4 copy-start
  885.4 99.5 %all-gather.11.cloned.1.call-start = ((), (), s32[]{:S(2)}) async-start(), calls=%async_computation.3 | async-start | bytes 3981312 | tf_op jit(solution)/shard_map/all_gather | solution.py:61
  896.5 140.7 %all-gather.9.cloned.1.call-start = ((), (), s32[]{:S(2)}) async-start(), calls=%async_computation.2 | async-start | bytes 3981312 | tf_op jit(solution)/shard_map/all_gather | solution.py:61
  907.3 182.3 %all-gather.7.cloned.1.call-start = ((), (), s32[]{:S(2)}) async-start(), calls=%async_computation.1 | async-start | bytes 3981312 | tf_op jit(solution)/shard_map/all_gather | solution.py:61
Sparse Core Ops, SparseCore 0:
  21.2 836.6 all-reduce.2
  885.5 46.7 all-gather.4
  934.6 50.2 all-gather.10
  987.0 50.2 all-gather.8
  1039.4 50.2 all-gather.6
